TPU v7x, 256 devices: a whole 4x4x8 slice. The times are simulated.
256 devices in a mesh: ctx: 32 (over x_lo, z, core), exp: 8 (over x_hi, y).
Axes of the slice: x: 4 (x_hi: 2, x_lo: 2; x = x_hi * 2 + x_lo), y: 4, z: 8, core: 2. Of those that a mesh axis runs over, the one named last changes fastest.
Arguments:
- queries: bfloat16 [8192, 8192], P('ctx', 'exp'), may hold values from -8 to 8
- keys: bfloat16 [8192, 512], P('ctx'), may hold values from -4 to 4
- values: bfloat16 [8192, 512], P('ctx'), may hold values from -6 to 6
- w_out: bfloat16 [8192, 4096], P('exp'), may hold values from -0.5 to 0.5
- residual: bfloat16 [8192, 4096], P(('ctx', 'exp')), may hold values from -1.5 to 1.5
- norm_gain: bfloat16 [4096], replicated, may hold values from 0.099609375 to 1.8984375
- expert_ids: int32 [8192, 2], P(('ctx', 'exp')), may hold values from 0 to 7, all different within a row; in each aligned block of 32 rows (0 to 31, 32 to 63, ...) at most 16 rows name the same one
- gate_weights: float32 [8192, 2], P(('ctx', 'exp')), may hold values from 0.2 to 1
- w_gate: bfloat16 [8, 4096, 768], P('exp', 'ctx'), may hold values from -0.09375 to 0.09375
- w_up: bfloat16 [8, 4096, 768], P('exp', 'ctx'), may hold values from -0.09375 to 0.09375
- w_down: bfloat16 [8, 768, 4096], P('exp', None, 'ctx'), may hold values from -0.21875 to 0.21875
Outputs:
- layer_out: bfloat16 [8192, 4096], P(('ctx', 'exp'))
Inputs may be any that keep to these rules, and one draw needn't show every extreme that they name: `expert_ids`: each row names 2 different experts; within each aligned block of 32 rows (the rows of one device) no expert is named by more than 16 rows.
All inputs are finite; a program needn't handle non-finite values.
Results may differ from a plain program's by a relative error of at most 0.025.
Values may be sent and summed in bfloat16 or wider, within the bound.
A program may use at most 128 MiB of HBM per device.

v0:
```python
import math
import jax
import jax.numpy as jnp
from jax import lax
from jax.sharding import PartitionSpec as P

D = 4096
HQ = 64
KVH = 4
HD = 128


def body(
    queries,
    keys,
    values,
    w_out,
    residual,
    norm_gain,
    expert_ids,
    gate_weights,
    w_gate,
    w_up,
    w_down,
):
    tok_rows = queries.shape[0]
    half_rows = tok_rows // 2
    exp_count = lax.axis_size("exp")
    heads_here = HQ // exp_count
    group = HQ // KVH
    kv_here = max(1, heads_here // group)
    heads_per_kv = heads_here // kv_here
    exp_index = lax.axis_index("exp")
    ctx_index = lax.axis_index("ctx")
    kv_first = exp_index * heads_here // group
    key_cols = lax.dynamic_slice_in_dim(keys, kv_first * HD, kv_here * HD, 1)
    value_cols = lax.dynamic_slice_in_dim(values, kv_first * HD, kv_here * HD, 1)
    scale = 1.0 / math.sqrt(HD)
    first_rows = queries[:half_rows]
    second_rows = queries[half_rows:]
    first_start = ctx_index * tok_rows
    second_start = ctx_index * tok_rows + half_rows
    query_sets = (
        first_rows.reshape(half_rows, kv_here, heads_per_kv, HD),
        second_rows.reshape(half_rows, kv_here, heads_per_kv, HD),
    )
    query_positions = (
        first_start + jnp.arange(half_rows, dtype=jnp.int32),
        second_start + jnp.arange(half_rows, dtype=jnp.int32),
    )
    last_positions = (first_start + half_rows - 1, second_start + half_rows - 1)

    def block_update(carry, query_four, query_pos, key_block, value_block, key_start):
        run_max, run_sum, run_acc = carry
        width = key_block.shape[0]
        key_three = key_block.reshape(width, kv_here, HD)
        value_three = value_block.reshape(width, kv_here, HD)
        scores = (
            jnp.einsum("tghd,kgd->ghtk", query_four, key_three, preferred_element_type=jnp.float32)
            * scale
        )
        key_pos = key_start + jnp.arange(width, dtype=jnp.int32)
        allowed = key_pos[None, :] <= query_pos[:, None]
        scores = jnp.where(allowed, scores, -1e30)
        new_max = jnp.maximum(run_max, jnp.max(scores, axis=-1))
        probs = jnp.where(allowed, jnp.exp(scores - new_max[..., None]), 0.0)
        factor = jnp.exp(run_max - new_max)
        run_sum = run_sum * factor + jnp.sum(probs, axis=-1)
        weighted = jnp.einsum(
            "ghtk,kgd->ghtd",
            probs.astype(jnp.bfloat16),
            value_three,
            preferred_element_type=jnp.float32,
        )
        run_acc = run_acc * factor[..., None] + weighted
        return (new_max, run_sum, run_acc)

    start_max = jnp.full((kv_here, heads_per_kv, half_rows), -1e30, jnp.float32)
    start_sum = jnp.zeros((kv_here, heads_per_kv, half_rows), jnp.float32)
    start_acc = jnp.zeros((kv_here, heads_per_kv, half_rows, HD), jnp.float32)
    start_state = (start_max, start_sum, start_acc)
    key_piece = lax.all_gather(key_cols, "ctx", axis=0, tiled=True)
    value_piece = lax.all_gather(value_cols, "ctx", axis=0, tiled=True)
    count = key_piece.shape[0]
    width = 512

    def one_block(index, inner):
        key_start = index * width
        key_block = lax.dynamic_slice_in_dim(key_piece, key_start, width, 0)
        value_block = lax.dynamic_slice_in_dim(value_piece, key_start, width, 0)
        updated = []
        for which in range(2):
            query_four = query_sets[which]
            query_pos = query_positions[which]
            updated.append(
                lax.cond(
                    key_start > last_positions[which],
                    lambda state: state,
                    lambda state: block_update(
                        state, query_four, query_pos, key_block, value_block, key_start
                    ),
                    inner[which],
                )
            )
        return (updated[0], updated[1])

    states = lax.fori_loop(0, count // width, one_block, (start_state, start_state))
    halves = []
    for which in range(2):
        run_max, run_sum, run_acc = states[which]
        halves.append(
            jnp.transpose(run_acc / run_sum[..., None], (2, 0, 1, 3))
            .reshape(half_rows, heads_here * HD)
            .astype(jnp.bfloat16)
        )
    attn_second = halves[1]
    attn = jnp.concatenate([halves[0], attn_second], axis=0)
    projected = lax.psum_scatter(
        jnp.dot(attn, w_out, preferred_element_type=jnp.float32).astype(jnp.bfloat16),
        "exp",
        scatter_dimension=0,
        tiled=True,
    ).astype(jnp.float32)
    hidden_state = (residual.astype(jnp.float32) + projected).astype(jnp.bfloat16)
    state_f = hidden_state.astype(jnp.float32)
    inv_rms = 1.0 / jnp.sqrt(jnp.mean(state_f * state_f, axis=1, keepdims=True) + 1e-06)
    normed = (state_f * inv_rms * norm_gain.astype(jnp.float32)[None, :]).astype(jnp.bfloat16)
    rows_here = expert_ids.shape[0]
    top_count = expert_ids.shape[1]
    experts_all = w_gate.shape[0] * exp_count
    capacity = min(rows_here, 2 * rows_here * top_count // experts_all)
    flat_ids = expert_ids.reshape(-1)
    onehot = (flat_ids[:, None] == jnp.arange(experts_all, dtype=jnp.int32)[None, :]).astype(
        jnp.int32
    )
    earlier = jnp.cumsum(onehot, axis=0) - onehot
    slot_index = jnp.sum(earlier * onehot, axis=1)
    target = flat_ids * capacity + slot_index
    picks = target[:, None] == jnp.arange(experts_all * capacity, dtype=jnp.int32)[None, :]
    dispatch_table = jnp.any(
        picks.reshape(rows_here, top_count, experts_all * capacity), axis=1
    ).astype(jnp.bfloat16)
    outgoing = jnp.einsum(
        "rs,rd->sd", dispatch_table, normed, preferred_element_type=jnp.float32
    ).astype(jnp.bfloat16)
    arrived = lax.all_to_all(
        outgoing.reshape(experts_all, capacity, D), "exp", split_axis=0, concat_axis=0, tiled=True
    )
    slot_rows = arrived.reshape(experts_all * capacity, D)
    gate_local = w_gate[0]
    up_local = w_up[0]
    gate_pre = jnp.dot(
        slot_rows,
        lax.all_gather(gate_local, "ctx", axis=0, tiled=True),
        preferred_element_type=jnp.float32,
    )
    up_pre = jnp.dot(
        slot_rows,
        lax.all_gather(up_local, "ctx", axis=0, tiled=True),
        preferred_element_type=jnp.float32,
    )
    expert_hidden = (jax.nn.silu(gate_pre) * up_pre).astype(jnp.bfloat16)
    down_local = w_down[0]
    expert_result = jnp.dot(
        expert_hidden,
        lax.all_gather(down_local, "ctx", axis=1, tiled=True),
        preferred_element_type=jnp.float32,
    ).astype(jnp.bfloat16)
    returned = lax.all_to_all(
        expert_result.reshape(experts_all, capacity, D),
        "exp",
        split_axis=0,
        concat_axis=0,
        tiled=True,
    )
    returned_flat = returned.reshape(experts_all * capacity, D)
    picked = jnp.dot(picks.astype(jnp.bfloat16), returned_flat, preferred_element_type=jnp.float32)
    weighted = gate_weights[:, :, None] * picked.reshape(rows_here, top_count, D)
    return (state_f + jnp.sum(weighted, axis=1)).astype(jnp.bfloat16)


def solution(mesh):
    placed = (
        P("ctx", "exp"),
        P("ctx", None),
        P("ctx", None),
        P("exp", None),
        P(("ctx", "exp"), None),
        P(),
        P(("ctx", "exp"), None),
        P(("ctx", "exp"), None),
        P("exp", "ctx", None),
        P("exp", "ctx", None),
        P("exp", None, "ctx"),
    )
    return jax.shard_map(
        body, mesh=mesh, in_specs=placed, out_specs=P(("ctx", "exp"), None), check_vma=False
    )
```

profile of v0, /device:TPU:2, one launch (start us, length us, event | category | flops | bytes accessed | tf_op | source)
XLA Modules:
  0.0 573.4 jit_solution(10112256670926563452)
XLA Ops:
  8.2 1.5 constant_dynamic-slice_fusion.3
  9.7 1.1 fusion.83
  11.5 64.9 %all-gather.11.cloned.1.call-done = bf16[8192,128]{1,0:T(8,128)(2,1)} async-done(((bf16[256,128]{1,0:T(8,128)(2,1)}), bf16[8192,128]{1,0:T(8,128)(2,1)}) %all-gather.11.cloned.1.call-update) | async-done | bytes 2097168 | tf_op jit(solution)/shard_map/all_gather | solution.py:83
  76.4 66.3 %all-gather.9.cloned.1.call-done = bf16[8192,128]{1,0:T(8,128)(2,1)} async-done(((bf16[256,128]{1,0:T(8,128)(2,1)}), bf16[8192,128]{1,0:T(8,128)(2,1)}) %all-gather.9.cloned.1.call-update) | async-done | bytes 2097168 | tf_op jit(solution)/shard_map/all_gather | solution.py:82
  142.8 54.4 %while.24 = (s32[]{:T(128)}, f32[1,8,128]{2,1,0:T(8,128)S(1)}, f32[1,8,128]{2,1,0:T(8,128)S(1)}, f32[1,8,128,128]{3,2,1,0:T(8,128)S(1)}, f32[1,8,128]{2,1,0:T(8,...) while((s32[]{:T(128)}, f32[1,8,128]{2,1,0:T(8,128)S(1)}, ...), condition=%wide.region_9.10_spmd.clone, body=%wide.region_0.9_spmd.clone.sunk | while | flops 551165184 | bytes 16921084 | solution.py:107
  142.8 1.0 constant_dynamic-slice_fusion.5
  143.8 2.0 conditional.7
  145.9 2.0 conditional.6
  148.0 1.0 constant_dynamic-slice_fusion.5
  149.0 2.0 conditional.7
  151.1 2.0 conditional.6
  153.1 1.0 constant_dynamic-slice_fusion.5
  154.1 2.0 conditional.7
  156.2 2.0 conditional.6
  158.3 1.0 constant_dynamic-slice_fusion.5
  159.3 2.0 conditional.7
  161.4 2.0 conditional.6
  163.4 1.0 constant_dynamic-slice_fusion.5
  164.5 2.0 conditional.7
  166.5 2.0 conditional.6
  168.6 1.0 constant_dynamic-slice_fusion.5
  169.6 2.0 conditional.7
  171.7 2.0 conditional.6
  173.8 1.0 constant_dynamic-slice_fusion.5
  174.8 2.0 conditional.7
  176.8 2.0 conditional.6
  178.9 1.0 constant_dynamic-slice_fusion.5
  179.9 2.0 conditional.7
  182.0 2.0 conditional.6
  184.1 1.0 constant_dynamic-slice_fusion.5
  185.1 2.0 conditional.7
  187.1 2.0 conditional.6
  189.2 1.0 constant_dynamic-slice_fusion.5
  190.4 1.0 constant_dynamic-slice_fusion.5
  191.5 1.0 constant_dynamic-slice_fusion.5
  192.7 1.0 constant_dynamic-slice_fusion.5
  195.0 1.0 constant_dynamic-slice_fusion.5
  197.8 7.1 %convolution_convert_fusion = bf16[256,4096]{1,0:T(8,128)(2,1)} fusion(bf16[1024,4096]{1,0:T(8,128)(2,1)} %param.20, bf16[128,1024]{0,1:T(8,128)(2,1)S(1)} %bitcast.139, bf16[128,1024]{0,1:T(8,128)(2,1)S(1)} %bitcast.138), kind=kOutput, calls=%fused_computation.64 | convolution fusion | flops 2149580800 | bytes 11010048 | tf_op jit(solution)/shard_map/dot_general | solution.py:119
  207.5 101.7 %reduce-scatter.2.cloned.1.call-done = bf16[32,4096]{1,0:T(8,128)(2,1)} async-done(((bf16[256,4096]{1,0:T(8,128)(2,1)}), bf16[32,4096]{1,0:T(8,128)(2,1)}) %reduce-scatter.2.cloned.1.call-update) | async-done | bytes 262160 | tf_op jit(solution)/shard_map/reduce_scatter | solution.py:118
  309.2 1.1 fusion.60
  310.3 1.5 convolution_convert_fusion.1
  311.8 25.3 %all_to_all.10 = bf16[8,16,4096]{2,1,0:T(8,128)(2,1)S(1)} all-to-all(bf16[8,16,4096]{2,1,0:T(8,128)(2,1)S(1)} %bitcast.130), channel_id=1, replica_groups=mesh['ctx'=32,'exp'=8] {'exp'}, dimensions={0} | all-to-all | bytes 2097152 | tf_op jit(solution)/shard_map/all_to_all | solution.py:146
  337.1 43.7 %all-gather.13.cloned.1.call-done = bf16[1,4096,768]{2,1,0:T(8,128)(2,1)} async-done(((bf16[1,128,768]{2,1,0:T(8,128)(2,1)}), bf16[1,4096,768]{2,1,0:T(8,128)(2,1)}) %all-gather.13.cloned.1.call-update) | async-done | bytes 6291472 | tf_op jit(solution)/shard_map/all_gather | solution.py:154
  380.8 3.8 fusion.46
  384.6 67.9 %all-gather.15.cloned.1.call-done = bf16[1,4096,768]{2,1,0:T(8,128)(2,1)} async-done(((bf16[1,128,768]{2,1,0:T(8,128)(2,1)}), bf16[1,4096,768]{2,1,0:T(8,128)(2,1)}) %all-gather.15.cloned.1.call-update) | async-done | bytes 6291472 | tf_op jit(solution)/shard_map/all_gather | solution.py:159
  452.5 82.3 %all-gather.17.cloned.1.call-done = bf16[1,768,4096]{2,1,0:T(8,128)(2,1)} async-done(((bf16[1,768,128]{2,1,0:T(8,128)(2,1)}), bf16[1,768,4096]{2,1,0:T(8,128)(2,1)}) %all-gather.17.cloned.1.call-update) | async-done | bytes 6291472 | tf_op jit(solution)/shard_map/all_gather | solution.py:166
  534.7 7.1 %fusion.48 = bf16[128,4096]{1,0:T(8,128)(2,1)S(1)} fusion(bf16[1,768,4096]{2,1,0:T(8,128)(2,1)} %all-gather.17.cloned.1.call-done, bf16[128,4096]{1,0:T(8,128)(2,1)S(1)} %bitcast.128, bf16[1,4096,768]{2,1,0:T(8,128)(2,1)} %all-gather.15.cloned.1.call-done, f32[128,768]{1,0:T(8,128)S(1)} %fusion.46), kind=kOutput, calls=%fused_computation.65 | convolution fusion | flops 1611726848 | bytes 15073280 | tf_op jit(solution)/shard_map/dot_general | solution.py:164
  541.8 23.5 %all_to_all.11 = bf16[8,16,4096]{2,1,0:T(8,128)(2,1)S(1)} all-to-all(bf16[8,16,4096]{2,1,0:T(8,128)(2,1)S(1)} %bitcast.129), channel_id=1, replica_groups=mesh['ctx'=32,'exp'=8] {'exp'}, dimensions={0} | all-to-all | bytes 2097152 | tf_op jit(solution)/shard_map/all_to_all | solution.py:169
  (290 shorter events, 44.6 us)
Async XLA Ops:
  6.5 1.0 copy-start
  6.5 69.9 %all-gather.11.cloned.1.call-start = ((), (), s32[]{:S(2)}) async-start(), calls=%async_computation.4 | async-start | bytes 2162688 | tf_op jit(solution)/shard_map/all_gather | solution.py:83
  8.1 134.5 %all-gather.9.cloned.1.call-start = ((), (), s32[]{:S(2)}) async-start(), calls=%async_computation.3 | async-start | bytes 2162688 | tf_op jit(solution)/shard_map/all_gather | solution.py:82
  9.7 299.5 %reduce-scatter.2.cloned.1.call-start = ((), (), s32[]{:S(2)}) async-start(), calls=%async_computation.5 | async-start | bytes 2359296 | tf_op jit(solution)/shard_map/reduce_scatter | solution.py:118
  204.8 1.8 copy-start.4
  204.8 2.5 copy-start.3
  204.8 104.3 %copy-start.1 = (bf16[32,4096]{1,0:T(8,128)(2,1)S(1)}, bf16[32,4096]{1,0:T(8,128)(2,1)}, u32[]{:S(2)}) copy-start(bf16[32,4096]{1,0:T(8,128)(2,1)} %param.21) | copy-start | bytes 786436
  204.9 176.0 %all-gather.13.cloned.1.call-start = ((), (), s32[]{:S(2)}) async-start(), calls=%async_computation.6 | async-start | bytes 6488064 | tf_op jit(solution)/shard_map/all_gather | solution.py:154
  205.4 247.0 %all-gather.15.cloned.1.call-start = ((), (), s32[]{:S(2)}) async-start(), calls=%async_computation.7 | async-start | bytes 6488064 | tf_op jit(solution)/shard_map/all_gather | solution.py:159
  206.0 328.7 %all-gather.17.cloned.1.call-start = ((), (), s32[]{:S(2)}) async-start(), calls=%async_computation.8 | async-start | bytes 6488064 | tf_op jit(solution)/shard_map/all_gather | solution.py:166
  541.8 23.6 %copy-start.5 = (f32[32,2]{0,1:T(2,128)S(1)}, f32[32,2]{0,1:T(2,128)}, u32[]{:S(2)}) copy-start(f32[32,2]{0,1:T(2,128)} %param.24) | copy-start | bytes 772
  541.8 23.9 %copy-start.2 = (bf16[32,4096]{1,0:T(8,128)(2,1)S(1)}, bf16[32,4096]{1,0:T(8,128)(2,1)}, u32[]{:S(2)}) copy-start(bf16[32,4096]{1,0:T(8,128)(2,1)} %reduce-scatter.2.cloned.1.call-done) | copy-start | bytes 786436
Sparse Core Ops, SparseCore 0:
  9.2 67.1 all-gather.10
  78.3 64.3 all-gather.8
  205.0 104.1 reduce-scatter.1
  310.9 69.8 all-gather.12
  382.5 69.9 all-gather.14
  454.1 80.5 all-gather.16
where the time goes:
time: 574 us; the launch traced here: 573 us
  waiting for transfers between devices  428 us (75%)
  blocking collectives  48.9 us (9%)
  matrix products  42.9 us (7%)
  local copies, waits for them, and re-layouts  21.8 us (4%)
  other arithmetic  14.7 us (3%)
  between operations  13.7 us (2%)
    reduce_scatter x1, waiting for transfers between devices, body(): lax.psum_scatter(jnp.dot(attn, w_out, preferred_element_type=jnp.float32)...  102 us
    all_gather x1, waiting for transfers between devices, body(): lax.all_gather(down_local, 'ctx', axis=1, tiled=True)  82.3 us
    all_gather x1, waiting for transfers between devices, body(): lax.all_gather(up_local, 'ctx', axis=0, tiled=True)  67.9 us
    all_gather x1, waiting for transfers between devices, body(): key_piece = lax.all_gather(key_cols, 'ctx', axis=0, tiled=True)  66.3 us
    all_gather x1, waiting for transfers between devices, body(): value_piece = lax.all_gather(value_cols, 'ctx', axis=0, tiled=True)  64.9 us
    all_gather x1, waiting for transfers between devices, body(): lax.all_gather(gate_local, 'ctx', axis=0, tiled=True)  43.7 us
    all_to_all x1, blocking collectives, body(): lax.all_to_all(outgoing.reshape(experts_all, capacity, D), 'exp', split_a...  25.3 us
    all_to_all x1, blocking collectives, body(): lax.all_to_all(expert_result.reshape(experts_all, capacity, D), 'exp', sp...  23.5 us
  transfers between devices with their start and end apart: 6, of which 6 were waited for; matrix products, arithmetic and copies ran while one was open for 2% of the time, Pallas kernels for 0%

commit v1 on v0

--- a/solution.py
+++ b/solution.py
@@ -163,7 +163,9 @@
     down_local = w_down[0]
     expert_result = jnp.dot(
         expert_hidden,
-        lax.all_gather(down_local, "ctx", axis=1, tiled=True),
+        jnp.concatenate(
+            lax.all_to_all(jnp.stack([down_local] * lax.axis_size("ctx")), "ctx", 0, 0), axis=1
+        ),
         preferred_element_type=jnp.float32,
     ).astype(jnp.bfloat16)
     returned = lax.all_to_all(

time: 574 us -> 583 us (1.016)
  blocking collectives: 48.9 us -> 22.5 us
  waiting for transfers between devices: 428 us -> 448 us
  starting transfers between devices: 0.2 us -> 11.1 us
    all_to_all x0 -> x2, waiting for transfers between devices: none -> 120 us  [the longest x1 97.4 us: body(): lax.all_to_all(jnp.stack([down_local] * lax.axis_size('ctx')), 'ctx', 0, 0)]
    all_gather x1 -> x0, waiting for transfers between devices: 82.3 us -> none  [body(): lax.all_gather(down_local, 'ctx', axis=1, tiled=True)]
    all_gather x1, waiting for transfers between devices: 67.9 us -> 21.8 us  [body(): lax.all_gather(up_local, 'ctx', axis=0, tiled=True)]
    all_gather x1, waiting for transfers between devices: 43.7 us -> 71.5 us  [body(): lax.all_gather(gate_local, 'ctx', axis=0, tiled=True)]
    all_to_all x1 -> x0, blocking collectives: 25.3 us -> none  [body(): lax.all_to_all(outgoing.reshape(experts_all, capacity, D), 'exp', split_a...]
    all_to_all x0 -> x2, starting transfers between devices: none -> 10.7 us  [the longest x1 6.16 us: body(): lax.all_to_all(jnp.stack([down_local] * lax.axis_size('ctx')), 'ctx', 0, 0)]
  transfers between devices with their start and end apart: 6 -> 7, of which waited for: 6 -> 7; matrix products, arithmetic and copies ran while one was open for 2% -> 3% of each run, Pallas kernels for 0% -> 0%
where the time goes in v1:
time: 583 us; the launch traced here: 582 us
  waiting for transfers between devices  448 us (77%)
  matrix products  44.5 us (8%)
  local copies, waits for them, and re-layouts  25.3 us (4%)
  blocking collectives  22.5 us (4%)
  other arithmetic  14.7 us (3%)
  between operations  13.4 us (2%)
  starting transfers between devices  11.1 us (2%)
    reduce_scatter x1, waiting for transfers between devices, body(): lax.psum_scatter(jnp.dot(attn, w_out, preferred_element_type=jnp.float32)...  103 us
    all_to_all x1, waiting for transfers between devices, body(): lax.all_to_all(jnp.stack([down_local] * lax.axis_size('ctx')), 'ctx', 0, 0)  97.4 us
    all_gather x1, waiting for transfers between devices, body(): lax.all_gather(gate_local, 'ctx', axis=0, tiled=True)  71.5 us
    all_gather x1, waiting for transfers between devices, body(): value_piece = lax.all_gather(value_cols, 'ctx', axis=0, tiled=True)  66.3 us
    all_gather x1, waiting for transfers between devices, body(): key_piece = lax.all_gather(key_cols, 'ctx', axis=0, tiled=True)  64.9 us
    all_to_all x1, blocking collectives, body(): lax.all_to_all(expert_result.reshape(experts_all, capacity, D), 'exp', sp...  22.5 us
    all_to_all x1, waiting for transfers between devices, body(): lax.all_to_all(outgoing.reshape(experts_all, capacity, D), 'exp', split_a...  22.4 us
    all_gather x1, waiting for transfers between devices, body(): lax.all_gather(up_local, 'ctx', axis=0, tiled=True)  21.8 us
  transfers between devices with their start and end apart: 7, of which 7 were waited for; matrix products, arithmetic and copies ran while one was open for 3% of the time, Pallas kernels for 0%

profile of v1, /device:TPU:2, one launch (start us, length us, event | category | flops | bytes accessed | tf_op | source)
XLA Modules:
  0.0 582.4 jit_solution(4365203806504898888)
XLA Ops:
  8.2 1.5 constant_dynamic-slice_fusion.2
  9.7 1.1 fusion.78
  11.5 64.9 %all-gather.7.cloned.1.call-done = bf16[8192,128]{1,0:T(8,128)(2,1)} async-done(((bf16[256,128]{1,0:T(8,128)(2,1)}), bf16[8192,128]{1,0:T(8,128)(2,1)}) %all-gather.7.cloned.1.call-update) | async-done | bytes 2097168 | tf_op jit(solution)/shard_map/all_gather | solution.py:82
  76.4 66.3 %all-gather.9.cloned.1.call-done = bf16[8192,128]{1,0:T(8,128)(2,1)} async-done(((bf16[256,128]{1,0:T(8,128)(2,1)}), bf16[8192,128]{1,0:T(8,128)(2,1)}) %all-gather.9.cloned.1.call-update) | async-done | bytes 2097168 | tf_op jit(solution)/shard_map/all_gather | solution.py:83
  142.8 54.4 %while.24 = (s32[]{:T(128)}, f32[1,8,128]{2,1,0:T(8,128)S(1)}, f32[1,8,128]{2,1,0:T(8,128)S(1)}, f32[1,8,128,128]{3,2,1,0:T(8,128)S(1)}, f32[1,8,128]{2,1,0:T(8,...) while((s32[]{:T(128)}, f32[1,8,128]{2,1,0:T(8,128)S(1)}, ...), condition=%wide.region_9.10_spmd.clone, body=%wide.region_0.9_spmd.clone.sunk | while | flops 551165184 | bytes 16921084 | solution.py:107
  142.8 1.0 constant_dynamic-slice_fusion.5
  143.8 2.0 conditional.7
  145.9 2.0 conditional.6
  148.0 1.0 constant_dynamic-slice_fusion.5
  149.0 2.0 conditional.7
  151.1 2.0 conditional.6
  153.1 1.0 constant_dynamic-slice_fusion.5
  154.1 2.0 conditional.7
  156.2 2.0 conditional.6
  158.3 1.0 constant_dynamic-slice_fusion.5
  159.3 2.0 conditional.7
  161.4 2.0 conditional.6
  163.4 1.0 constant_dynamic-slice_fusion.5
  164.5 2.0 conditional.7
  166.5 2.0 conditional.6
  168.6 1.0 constant_dynamic-slice_fusion.5
  169.6 2.0 conditional.7
  171.7 2.0 conditional.6
  173.8 1.0 constant_dynamic-slice_fusion.5
  174.8 2.0 conditional.7
  176.8 2.0 conditional.6
  178.9 1.0 constant_dynamic-slice_fusion.5
  179.9 2.0 conditional.7
  182.0 2.0 conditional.6
  184.1 1.0 constant_dynamic-slice_fusion.5
  185.1 2.0 conditional.7
  187.1 2.0 conditional.6
  189.2 1.0 constant_dynamic-slice_fusion.5
  190.4 1.0 constant_dynamic-slice_fusion.5
  197.8 7.1 %convolution_convert_fusion = bf16[256,4096]{1,0:T(8,128)(2,1)} fusion(bf16[1024,4096]{1,0:T(8,128)(2,1)} %param.20, bf16[128,1024]{0,1:T(8,128)(2,1)S(1)} %bitcast.138, bf16[128,1024]{0,1:T(8,128)(2,1)S(1)} %bitcast.137), kind=kOutput, calls=%fused_computation.62 | convolution fusion | flops 2149580800 | bytes 11010048 | tf_op jit(solution)/shard_map/dot_general | solution.py:119
  206.4 102.8 %reduce-scatter.2.cloned.1.call-done = bf16[32,4096]{1,0:T(8,128)(2,1)} async-done(((bf16[256,4096]{1,0:T(8,128)(2,1)}), bf16[32,4096]{1,0:T(8,128)(2,1)}) %reduce-scatter.2.cloned.1.call-update) | async-done | bytes 262160 | tf_op jit(solution)/shard_map/reduce_scatter | solution.py:118
  309.2 1.1 fusion.55
  310.4 2.4 convolution_convert_fusion.2
  312.8 4.6 all-to-all-start
  317.6 22.4 %all-to-all-done = bf16[8,16,4096]{2,1,0:T(8,128)(2,1)S(1)} async-done(((bf16[8,16,4096]{2,1,0:T(8,128)(2,1)}), bf16[8,16,4096]{2,1,0:T(8,128)(2,1)S(1)}, u32[]{:S(2)}, u32[]{:S(2)}) %all-to-all-start) | async-done | bytes 1048608 | tf_op jit(solution)/shard_map/all_to_all | solution.py:146
  339.9 3.3 stack.3
  343.2 6.2 %all-to-all-start.1 = ((bf16[32,768,128]{1,2,0:T(8,128)(2,1)}), bf16[32,768,128]{1,2,0:T(8,128)(2,1)}, u32[]{:S(2)}, u32[]{:S(2)}) async-start(bf16[32,768,128]{1,2,0:T(8,128)(2,1)} %stack.3), calls=%async_computation.2 | async-start | bytes 12582912 | tf_op jit(solution)/shard_map/all_to_all | solution.py:167
  350.0 71.5 %all-gather.11.cloned.1.call-done = bf16[1,4096,768]{2,1,0:T(8,128)(2,1)} async-done(((bf16[1,128,768]{2,1,0:T(8,128)(2,1)}), bf16[1,4096,768]{2,1,0:T(8,128)(2,1)}) %all-gather.11.cloned.1.call-update) | async-done | bytes 6291472 | tf_op jit(solution)/shard_map/all_gather | solution.py:154
  421.5 3.8 fusion.44
  425.3 97.4 %all-to-all-done.1 = bf16[32,768,128]{1,2,0:T(8,128)(2,1)} async-done(((bf16[32,768,128]{1,2,0:T(8,128)(2,1)}), bf16[32,768,128]{1,2,0:T(8,128)(2,1)}, u32[]{:S(2)}, u32[]{:S(2)}) %all-to-all-start.1) | async-done | bytes 6291488 | tf_op jit(solution)/shard_map/all_to_all | solution.py:167
  522.7 21.8 %all-gather.13.cloned.1.call-done = bf16[1,4096,768]{2,1,0:T(8,128)(2,1)} async-done(((bf16[1,128,768]{2,1,0:T(8,128)(2,1)}), bf16[1,4096,768]{2,1,0:T(8,128)(2,1)}) %all-gather.13.cloned.1.call-update) | async-done | bytes 6291472 | tf_op jit(solution)/shard_map/all_gather | solution.py:159
  544.5 7.7 %convolution_convert_fusion.1 = bf16[128,4096]{1,0:T(8,128)(2,1)S(1)} fusion(bf16[768,4096]{0,1:T(8,128)(2,1)} %bitcast.37, bf16[128,4096]{1,0:T(8,128)(2,1)S(1)} %bitcast.128, bf16[1,4096,768]{2,1,0:T(8,128)(2,1)} %all-gather.13.cloned.1.call-done, f32[128,768]{1,0:T(8,128)S(1)} %fusion.44), kind=kOutput, calls=%fused_computation.63 | convolution fusion | flops 1611726848 | bytes 15073280 | tf_op jit(solution)/shard_map/dot_general | solution.py:164
  552.2 22.5 %all_to_all.15 = bf16[8,16,4096]{2,1,0:T(8,128)(2,1)S(1)} all-to-all(bf16[8,16,4096]{2,1,0:T(8,128)(2,1)S(1)} %bitcast.129), channel_id=1, replica_groups=mesh['ctx'=32,'exp'=8] {'exp'}, dimensions={0} | all-to-all | bytes 2097152 | tf_op jit(solution)/shard_map/all_to_all | solution.py:171
  (294 shorter events, 47.2 us)
Async XLA Ops:
  6.5 1.0 copy-start
  6.5 69.9 %all-gather.7.cloned.1.call-start = ((), (), s32[]{:S(2)}) async-start(), calls=%async_computation.4 | async-start | bytes 2162688 | tf_op jit(solution)/shard_map/all_gather | solution.py:82
  8.1 134.5 %all-gather.9.cloned.1.call-start = ((), (), s32[]{:S(2)}) async-start(), calls=%async_computation.5 | async-start | bytes 2162688 | tf_op jit(solution)/shard_map/all_gather | solution.py:83
  9.7 299.6 %reduce-scatter.2.cloned.1.call-start = ((), (), s32[]{:S(2)}) async-start(), calls=%async_computation.6 | async-start | bytes 2359296 | tf_op jit(solution)/shard_map/reduce_scatter | solution.py:118
  204.9 0.7 copy-start.5
  204.9 1.4 copy-start.4
  204.9 104.4 %copy-start.1 = (bf16[32,4096]{1,0:T(8,128)(2,1)S(1)}, bf16[32,4096]{1,0:T(8,128)(2,1)}, u32[]{:S(2)}) copy-start(bf16[32,4096]{1,0:T(8,128)(2,1)} %param.21) | copy-start | bytes 786436
  204.9 216.6 %all-gather.11.cloned.1.call-start = ((), (), s32[]{:S(2)}) async-start(), calls=%async_computation.7 | async-start | bytes 6488064 | tf_op jit(solution)/shard_map/all_gather | solution.py:154
  206.4 111.0 %copy-start.3 = (bf16[1,768,128]{2,1,0:T(8,128)(2,1)S(1)}, bf16[1,768,128]{2,1,0:T(8,128)(2,1)}, u32[]{:S(2)}) copy-start(bf16[1,768,128]{2,1,0:T(8,128)(2,1)} %param.27) | copy-start | bytes 589828
  312.8 27.1 %all-to-all-start = ((bf16[8,16,4096]{2,1,0:T(8,128)(2,1)}), bf16[8,16,4096]{2,1,0:T(8,128)(2,1)S(1)}, u32[]{:S(2)}, u32[]{:S(2)}) async-start(bf16[8,16,4096]{2,1,0:T(8,128)(2,1)} %bitcast.31), calls=%async_computation.1 | async-start | bytes 2097152 | tf_op jit(solution)/shard_map/all_to_all | solution.py:146
  343.2 179.4 %all-to-all-start.1 = ((bf16[32,768,128]{1,2,0:T(8,128)(2,1)}), bf16[32,768,128]{1,2,0:T(8,128)(2,1)}, u32[]{:S(2)}, u32[]{:S(2)}) async-start(bf16[32,768,128]{1,2,0:T(8,128)(2,1)} %stack.3), calls=%async_computation.2 | async-start | bytes 12582912 | tf_op jit(solution)/shard_map/all_to_all | solution.py:167
  349.4 195.1 %all-gather.13.cloned.1.call-start = ((), (), s32[]{:S(2)}) async-start(), calls=%async_computation.8 | async-start | bytes 6488064 | tf_op jit(solution)/shard_map/all_gather | solution.py:159
  552.2 22.5 %copy-start.6 = (f32[32,2]{0,1:T(2,128)S(1)}, f32[32,2]{0,1:T(2,128)}, u32[]{:S(2)}) copy-start(f32[32,2]{0,1:T(2,128)} %param.24) | copy-start | bytes 772
  552.2 22.8 %copy-start.2 = (bf16[32,4096]{1,0:T(8,128)(2,1)S(1)}, bf16[32,4096]{1,0:T(8,128)(2,1)}, u32[]{:S(2)}) copy-start(bf16[32,4096]{1,0:T(8,128)(2,1)} %reduce-scatter.2.cloned.1.call-done) | copy-start | bytes 786436
Sparse Core Ops, SparseCore 0:
  9.2 67.1 all-gather.6
  78.3 64.3 all-gather.8
  205.0 104.1 reduce-scatter.1
  311.0 110.4 all-gather.10
  423.2 121.2 all-gather.12
